TPU v7x, 512 devices: a whole 4x4x16 slice. The times are simulated.
512 devices in a mesh: dp: 2 (over x_lo), seq: 32 (over z, core), tensor: 8 (over y, x_hi).
Axes of the slice: x: 4 (x_hi: 2, x_lo: 2; x = x_hi * 2 + x_lo), y: 4, z: 16, core: 2. Of those that a mesh axis runs over, the one named last changes fastest.
Arguments:
- queries: bfloat16 [2, 4096, 3072], P('dp', 'seq', 'tensor'), may hold values from -24 to 24
- keys: bfloat16 [2, 8192, 3072], P('dp', 'seq', 'tensor'), may hold values from -8 to 8
- values: bfloat16 [2, 8192, 3072], P('dp', 'seq', 'tensor'), may hold values from -160 to 160
- grad_out: bfloat16 [2, 4096, 3072], P('dp', 'seq', 'tensor'), may hold values from -60 to 60
- gain: float32 [3072], P('tensor'), may hold values from 0.1 to 1.9
- band_start: int32 [2, 32], P('dp', 'seq'), may hold values from 0 to 62, as said below
- band_end: int32 [2, 32], P('dp', 'seq'), may hold values from 6 to 64
Outputs:
- attended: bfloat16 [2, 4096, 3072], P('dp', 'seq', 'tensor')
- grad_queries: bfloat16 [2, 4096, 3072], P('dp', 'seq', 'tensor')
- grad_keys: bfloat16 [2, 8192, 3072], P('dp', 'seq', 'tensor')
- grad_values: bfloat16 [2, 8192, 3072], P('dp', 'seq', 'tensor')
- grad_gain: float32 [3072], P('tensor')
Inputs may be any that keep to these rules, and one draw needn't show every extreme that they name: Along the token blocks of a recording band_start and band_end never fall and band_start < band_end; the band of a token block held by seq index j lies within encoder blocks (j - 2) * (2) to (j + 3) * 2 - 1, and in every draw some bands reach both of these limits.
All inputs are finite; a program needn't handle non-finite values.
Results may differ from a plain program's by a relative error of at most 0.008.
Values may be sent and summed in bfloat16 or wider, within the bound.
No kernel may reach another device: no remote copies, remote signals or barrier semaphores. Data moves between devices by JAX's collectives and lax.ppermute only.
A program may use at most 64 MiB of HBM per device.

v0:
```python
import jax
import jax.numpy as jnp
from jax import lax
from jax.sharding import PartitionSpec as P

D = 3072
HD = 96
TB = 128
EB = 128
REACH = 2
epsilon = 1e-06


def shifted(array, axis, by):
    size = lax.axis_size(axis)
    pairs = [(i, i + by) for i in range(size) if 0 <= i + by < size]
    return lax.ppermute(array, axis, pairs)


def head_probs(query_head, key_head, allowed, scale):
    scores = (
        lax.dot_general(
            query_head, key_head, (((1,), (1,)), ((), ())), preferred_element_type=jnp.float32
        )
        * scale
    )
    scores = jnp.where(allowed, scores, -jnp.inf)
    top = jnp.max(scores, axis=1, keepdims=True)
    weights = jnp.exp(scores - top)
    return weights / jnp.sum(weights, axis=1, keepdims=True)


def per_device(queries, keys, values, grad_out, gain, band_start, band_end):
    query_local = queries[0]
    key_local = keys[0]
    value_local = values[0]
    grad_local = grad_out[0].astype(jnp.float32)
    starts = band_start[0]
    ends = band_end[0]
    tok_rows, width = query_local.shape
    frame_rows = key_local.shape[0]
    heads = width // HD
    scale = HD ** (-0.5)
    here = lax.axis_index("seq")
    pair = jnp.stack([key_local, value_local])
    pieces = []
    for offset in range(-REACH, REACH + 1):
        if offset == 0:
            pieces.append(pair)
        else:
            pieces.append(shifted(pair, "seq", -offset))
    window = jnp.concatenate(pieces, axis=1)
    key_window = window[0]
    value_window = window[1]
    span = key_window.shape[0]
    frame_block = ((here - REACH) * frame_rows + jnp.arange(span, dtype=jnp.int32)) // EB
    row_start = jnp.repeat(starts, TB)
    row_end = jnp.repeat(ends, TB)
    allowed = (frame_block[None, :] >= row_start[:, None]) & (
        frame_block[None, :] < row_end[:, None]
    )
    outputs = []
    kept_probs = []
    for head in range(heads):
        columns = slice(head * HD, (head + 1) * HD)
        probs = head_probs(query_local[:, columns], key_window[:, columns], allowed, scale)
        kept_probs.append(probs)
        outputs.append(
            jnp.dot(
                probs.astype(jnp.bfloat16),
                value_window[:, columns],
                preferred_element_type=jnp.float32,
            )
        )
    attn = jnp.concatenate(outputs, axis=1)
    scaled_grad = grad_local * gain[None, :]
    square_local = jnp.sum(attn * attn, axis=1)
    cross_local = jnp.sum(scaled_grad * attn, axis=1)
    square_total = lax.psum(square_local, "tensor")
    inv_rms = lax.rsqrt(square_total / D + epsilon)
    normed = attn * inv_rms[:, None]
    attended = (normed * gain[None, :]).astype(jnp.bfloat16)
    cross_total = lax.psum(cross_local, "tensor")
    mean_cross = inv_rms * cross_total / D
    grad_attn = (inv_rms[:, None] * (scaled_grad - normed * mean_cross[:, None])).astype(
        jnp.bfloat16
    )
    grad_gain = lax.psum(jnp.sum(grad_local * normed, axis=0), ("dp", "seq"))
    query_grads = []
    key_grads = []
    value_grads = []
    for head in range(heads):
        columns = slice(head * HD, (head + 1) * HD)
        query_head = query_local[:, columns]
        key_head = key_window[:, columns]
        value_head = value_window[:, columns]
        grad_head = grad_attn[:, columns]
        probs = kept_probs[head]
        probs_b = probs.astype(jnp.bfloat16)
        grad_probs = lax.dot_general(
            grad_head, value_head, (((1,), (1,)), ((), ())), preferred_element_type=jnp.float32
        )
        inner = jnp.sum(probs * grad_probs, axis=1, keepdims=True)
        grad_scores = (probs * (grad_probs - inner)).astype(jnp.bfloat16)
        query_grads.append(
            scale * jnp.dot(grad_scores, key_head, preferred_element_type=jnp.float32)
        )
        key_grads.append(
            scale
            * lax.dot_general(
                grad_scores,
                query_head,
                (((0,), (0,)), ((), ())),
                preferred_element_type=jnp.float32,
            )
        )
        value_grads.append(
            lax.dot_general(
                probs_b, grad_head, (((0,), (0,)), ((), ())), preferred_element_type=jnp.float32
            )
        )
    grad_queries = jnp.concatenate(query_grads, axis=1).astype(jnp.bfloat16)
    window_grads = jnp.stack(
        [jnp.concatenate(key_grads, axis=1), jnp.concatenate(value_grads, axis=1)]
    )
    parts = [
        window_grads[:, index * frame_rows : (index + 1) * frame_rows]
        for index in range(2 * REACH + 1)
    ]
    total = parts[REACH]
    for offset in range(-REACH, REACH + 1):
        if offset != 0:
            total = total + shifted(
                parts[REACH + offset].astype(jnp.bfloat16), "seq", offset
            ).astype(jnp.float32)
    grad_keys = total[0].astype(jnp.bfloat16)
    grad_values = total[1].astype(jnp.bfloat16)
    return (attended[None], grad_queries[None], grad_keys[None], grad_values[None], grad_gain)


def solution(mesh):
    return jax.shard_map(
        per_device,
        mesh=mesh,
        in_specs=(
            P("dp", "seq", "tensor"),
            P("dp", "seq", "tensor"),
            P("dp", "seq", "tensor"),
            P("dp", "seq", "tensor"),
            P("tensor"),
            P("dp", "seq"),
            P("dp", "seq"),
        ),
        out_specs=(
            P("dp", "seq", "tensor"),
            P("dp", "seq", "tensor"),
            P("dp", "seq", "tensor"),
            P("dp", "seq", "tensor"),
            P("tensor"),
        ),
        check_vma=False,
    )
```

profile of v0, /device:TPU:6, one launch (start us, length us, event | category | flops | bytes accessed | tf_op | source)
XLA Modules:
  0.0 224.1 jit_solution(527827791470561601)
XLA Ops:
  0.7 1.0 constant_dynamic-update-slice_fusion.1
  1.7 1.0 constant_dynamic-update-slice_fusion
  2.6 3.8 %collective-permute-start = (bf16[2,256,384]{2,1,0:T(8,128)(2,1)S(1)}, bf16[2,256,384]{2,1,0:T(8,128)(2,1)S(1)}, u32[]{:S(2)}, u32[]{:S(2)}) collective-permute-start(bf16[2,256,384]{2,1,0:T(8,128)(2,1)S(1)} %constant_dynamic-update-slice_fusion), channel_id=1, source_target_pairs={{0,16},{8,24},{16,32},{24,40},{32,48},{40,56},{48,64},{56,72},{64,... | collective-permute-start | bytes 1179656 | tf_op jit(solution)/shard_map/ppermute | solution.py:17
  6.5 1.5 collective-permute-start.1
  8.0 1.3 collective-permute-start.2
  9.3 1.3 collective-permute-start.3
  11.9 1.0 copy.12
  12.9 3.0 %collective-permute-done = bf16[2,256,384]{2,1,0:T(8,128)(2,1)S(1)} collective-permute-done((bf16[2,256,384]{2,1,0:T(8,128)(2,1)S(1)}, bf16[2,256,384]{2,1,0:T(8,128)(2,1)S(1)}, u32[]{:S(2)}, u32[]{:S(2)}) %collective-permute-start) | collective-permute-done | bytes 393248 | tf_op jit(solution)/shard_map/ppermute | solution.py:17
  16.2 11.9 %collective-permute-done.3 = bf16[2,256,384]{2,1,0:T(8,128)(2,1)S(1)} collective-permute-done((bf16[2,256,384]{2,1,0:T(8,128)(2,1)S(1)}, bf16[2,256,384]{2,1,0:T(8,128)(2,1)S(1)}, u32[]{:S(2)}, u32[]{:S(2)}) %collective-permute-start.3) | collective-permute-done | bytes 393248 | tf_op jit(solution)/shard_map/ppermute | solution.py:17
  33.1 20.7 %psum.21 = f32[128]{0:T(128)S(1)} all-reduce(f32[128]{0:T(128)S(1)} %multiply_reduce_fusion), channel_id=1, replica_groups=mesh['dp'=2,'seq'=32,'tensor'=8] {'tensor'}, use_global_device_ids=true, to_apply=%region_9.10 | all-reduce | flops 128 | bytes 1024 | tf_op jit(solution)/shard_map/psum | solution.py:79
  54.1 23.3 %psum.22 = f32[128]{0:T(128)S(1)} all-reduce(f32[128]{0:T(128)S(1)} %get-tuple-element.11), channel_id=1, replica_groups=mesh['dp'=2,'seq'=32,'tensor'=8] {'tensor'}, use_global_device_ids=true, to_apply=%region_11.12 | all-reduce | flops 128 | bytes 1024 | tf_op jit(solution)/shard_map/psum | solution.py:83
  77.5 1.4 fusion.19
  79.3 1.2 fusion.23
  80.5 1.1 fusion.25
  83.1 1.2 convolution_multiply_fusion.5
  84.3 1.1 fusion.70
  85.3 1.1 fusion.69
  86.4 1.0 fusion.68
  87.4 1.1 fusion.67
  88.6 0.8 copy.21
  89.4 1.2 fusion.24
  91.8 0.9 copy-done.11
  93.6 0.9 copy-done
  94.5 1.0 fusion.98
  95.6 3.8 %collective-permute-start.7 = (bf16[2,256,384]{1,2,0:T(8,128)(2,1)}, bf16[2,256,384]{1,2,0:T(8,128)(2,1)S(1)}, u32[]{:S(2)}, u32[]{:S(2)}) collective-permute-start(bf16[2,256,384]{1,2,0:T(8,128)(2,1)} %get-tuple-element.13), channel_id=1, source_target_pairs={{0,16},{8,24},{16,32},{24,40},{32,48},{40,56},{48,64},{56,72},{64,... | collective-permute-start | bytes 1179656 | tf_op jit(solution)/shard_map/ppermute | solution.py:17
  99.4 2.1 collective-permute-start.6
  101.5 1.3 collective-permute-start.5
  102.8 1.3 collective-permute-start.4
  105.6 115.3 %psum.23 = f32[384]{0:T(512)} all-reduce(f32[384]{0:T(512)S(1)} %get-tuple-element.10), channel_id=1, replica_groups=mesh['dp'=2,'seq'=32,'tensor'=8] {'dp','seq'}, use_global_device_ids=true, to_apply=%region_17.18 | all-reduce | flops 384 | bytes 3072 | tf_op jit(solution)/shard_map/psum | solution.py:88
  220.9 1.6 fusion.18
  222.5 0.8 copy.23
  223.3 0.8 copy.24
  (79 shorter events, 11.2 us)
Async XLA Ops:
  0.6 15.4 %copy-start.7 = (bf16[1,256,384]{2,1,0:T(8,128)(2,1)S(1)}, bf16[1,256,384]{2,1,0:T(8,128)(2,1)}, u32[]{:S(2)}) copy-start(bf16[1,256,384]{2,1,0:T(8,128)(2,1)} %param.8) | copy-start | bytes 589828
  0.6 15.5 %copy-start.8 = (bf16[1,256,384]{2,1,0:T(8,128)(2,1)S(1)}, bf16[1,256,384]{2,1,0:T(8,128)(2,1)}, u32[]{:S(2)}) copy-start(bf16[1,256,384]{2,1,0:T(8,128)(2,1)} %param.9) | copy-start | bytes 589828
  2.6 13.3 %collective-permute-start = (bf16[2,256,384]{2,1,0:T(8,128)(2,1)S(1)}, bf16[2,256,384]{2,1,0:T(8,128)(2,1)S(1)}, u32[]{:S(2)}, u32[]{:S(2)}) collective-permute-start(bf16[2,256,384]{2,1,0:T(8,128)(2,1)S(1)} %constant_dynamic-update-slice_fusion), channel_id=1, source_target_pairs={{0,16},{8,24},{16,32},{24,40},{32,48},{40,56},{48,64},{56,72},{64,... | collective-permute-start | bytes 1179656 | tf_op jit(solution)/shard_map/ppermute | solution.py:17
  6.5 9.5 %collective-permute-start.1 = (bf16[2,256,384]{2,1,0:T(8,128)(2,1)S(1)}, bf16[2,256,384]{2,1,0:T(8,128)(2,1)S(1)}, u32[]{:S(2)}, u32[]{:S(2)}) collective-permute-start(bf16[2,256,384]{2,1,0:T(8,128)(2,1)S(1)} %constant_dynamic-update-slice_fusion), channel_id=1, source_target_pairs={{0,8},{8,16},{16,24},{24,32},{32,40},{40,48},{48,56},{56,64},{64,7... | collective-permute-start | bytes 1179656 | tf_op jit(solution)/shard_map/ppermute | solution.py:17
  8.0 8.2 %collective-permute-start.2 = (bf16[2,256,384]{2,1,0:T(8,128)(2,1)S(1)}, bf16[2,256,384]{2,1,0:T(8,128)(2,1)S(1)}, u32[]{:S(2)}, u32[]{:S(2)}) collective-permute-start(bf16[2,256,384]{2,1,0:T(8,128)(2,1)S(1)} %constant_dynamic-update-slice_fusion), channel_id=1, source_target_pairs={{8,0},{16,8},{24,16},{32,24},{40,32},{48,40},{56,48},{64,56},{72,6... | collective-permute-start | bytes 1179656 | tf_op jit(solution)/shard_map/ppermute | solution.py:17
  9.3 18.8 %collective-permute-start.3 = (bf16[2,256,384]{2,1,0:T(8,128)(2,1)S(1)}, bf16[2,256,384]{2,1,0:T(8,128)(2,1)S(1)}, u32[]{:S(2)}, u32[]{:S(2)}) collective-permute-start(bf16[2,256,384]{2,1,0:T(8,128)(2,1)S(1)} %constant_dynamic-update-slice_fusion), channel_id=1, source_target_pairs={{16,0},{24,8},{32,16},{40,24},{48,32},{56,40},{64,48},{72,56},{80,... | collective-permute-start | bytes 1179656 | tf_op jit(solution)/shard_map/ppermute | solution.py:17
  28.2 0.9 copy-start.9
  28.4 2.3 %copy-start.1 = (bf16[1280,384]{1,0:T(8,128)(2,1)}, bf16[1280,384]{1,0:T(8,128)(2,1)S(1)}, u32[]{:S(2)}) copy-start(bf16[1280,384]{1,0:T(8,128)(2,1)S(1)} %get-tuple-element.16) | copy-start | bytes 2949124
  28.4 4.3 %copy-start.5 = (bf16[1280,384]{1,0:T(8,128)(2,1)}, bf16[1280,384]{1,0:T(8,128)(2,1)S(1)}, u32[]{:S(2)}) copy-start(bf16[1280,384]{1,0:T(8,128)(2,1)S(1)} %get-tuple-element.17) | copy-start | bytes 2949124
  32.5 21.3 %copy-start.15 = (f32[384]{0:T(512)S(1)}, f32[384]{0:T(512)}, u32[]{:S(2)}) copy-start(f32[384]{0:T(512)} %param.11) | copy-start | bytes 4612
  77.3 1.6 copy-start.6
  80.5 1.3 copy-start.2
  88.5 2.5 %copy-start.10 = (f32[128,1280]{0,1:T(8,128)S(1)}, f32[128,1280]{0,1:T(8,128)}, u32[]{:S(2)}) copy-start(f32[128,1280]{0,1:T(8,128)} %get-tuple-element.35) | copy-start | bytes 1966084
  90.6 1.0 copy-start.4
  91.6 1.0 copy-start.11
  91.6 1.2 copy-start.12
  91.6 1.3 copy-start.13
  91.6 1.5 copy-start.14
  93.2 1.3 copy-start
  94.5 9.5 %copy-start.3 = (bf16[1280,384]{1,0:T(8,128)(2,1)S(1)}, bf16[1280,384]{1,0:T(8,128)(2,1)}, u32[]{:S(2)}) copy-start(bf16[1280,384]{1,0:T(8,128)(2,1)} %copy-done.1) | copy-start | bytes 2949124
  95.6 125.3 %collective-permute-start.7 = (bf16[2,256,384]{1,2,0:T(8,128)(2,1)}, bf16[2,256,384]{1,2,0:T(8,128)(2,1)S(1)}, u32[]{:S(2)}, u32[]{:S(2)}) collective-permute-start(bf16[2,256,384]{1,2,0:T(8,128)(2,1)} %get-tuple-element.13), channel_id=1, source_target_pairs={{0,16},{8,24},{16,32},{24,40},{32,48},{40,56},{48,64},{56,72},{64,... | collective-permute-start | bytes 1179656 | tf_op jit(solution)/shard_map/ppermute | solution.py:17
  99.4 121.4 %collective-permute-start.6 = (bf16[2,256,384]{1,2,0:T(8,128)(2,1)}, bf16[2,256,384]{1,2,0:T(8,128)(2,1)}, u32[]{:S(2)}, u32[]{:S(2)}) collective-permute-start(bf16[2,256,384]{1,2,0:T(8,128)(2,1)} %get-tuple-element.14), channel_id=1, source_target_pairs={{0,8},{8,16},{16,24},{24,32},{32,40},{40,48},{48,56},{56,64},{64,7... | collective-permute-start | bytes 1179656 | tf_op jit(solution)/shard_map/ppermute | solution.py:17
  101.5 119.4 %collective-permute-start.5 = (bf16[2,256,384]{1,2,0:T(8,128)(2,1)}, bf16[2,256,384]{1,2,0:T(8,128)(2,1)}, u32[]{:S(2)}, u32[]{:S(2)}) collective-permute-start(bf16[2,256,384]{1,2,0:T(8,128)(2,1)} %get-tuple-element.15), channel_id=1, source_target_pairs={{8,0},{16,8},{24,16},{32,24},{40,32},{48,40},{56,48},{64,56},{72,6... | collective-permute-start | bytes 1179656 | tf_op jit(solution)/shard_map/ppermute | solution.py:17
  102.8 118.1 %collective-permute-start.4 = (bf16[2,256,384]{1,2,0:T(8,128)(2,1)S(1)}, bf16[2,256,384]{1,2,0:T(8,128)(2,1)}, u32[]{:S(2)}, u32[]{:S(2)}) collective-permute-start(bf16[2,256,384]{1,2,0:T(8,128)(2,1)S(1)} %get-tuple-element.12), channel_id=1, source_target_pairs={{16,0},{24,8},{32,16},{40,24},{48,32},{56,40},{64,48},{72,56},{80,... | collective-permute-start | bytes 1179656 | tf_op jit(solution)/shard_map/ppermute | solution.py:17
where the time goes:
time: 225 us; the launch traced here: 224 us
  blocking collectives  159 us (71%)
  starting transfers between devices  16.4 us (7%)
  matrix products  15.2 us (7%)
  waiting for transfers between devices  14.9 us (7%)
  local copies, waits for them, and re-layouts  10.8 us (5%)
  other arithmetic  5.26 us (2%)
  between operations  2.34 us (1%)
    psum x1, blocking collectives, per_device(): grad_gain = lax.psum(jnp.sum(grad_local * normed, axis=0), ('dp', 'seq'))  115 us
    psum x1, blocking collectives, per_device(): cross_total = lax.psum(cross_local, 'tensor')  23.3 us
    psum x1, blocking collectives, per_device(): square_total = lax.psum(square_local, 'tensor')  20.7 us
    ppermute x8, starting transfers between devices, shifted(): return lax.ppermute(array, axis, pairs)  16.4 us
    ppermute x8, waiting for transfers between devices, shifted(): return lax.ppermute(array, axis, pairs)  14.9 us
    unnamed x43, local copies, waits for them, and re-layouts  8.52 us
  transfers between devices with their start and end apart: 8, of which 2 were waited for; matrix products, arithmetic and copies ran while one was open for 1% of the time, Pallas kernels for 0%

commit v1 on v0

--- a/solution.py
+++ b/solution.py
@@ -85,7 +85,7 @@
     grad_attn = (inv_rms[:, None] * (scaled_grad - normed * mean_cross[:, None])).astype(
         jnp.bfloat16
     )
-    grad_gain = lax.psum(jnp.sum(grad_local * normed, axis=0), ("dp", "seq"))
+    grad_gain = lax.psum(lax.psum(jnp.sum(grad_local * normed, axis=0), "dp"), "seq")
     query_grads = []
     key_grads = []
     value_grads = []

time: 225 us -> 168 us (0.75)
  blocking collectives: 159 us -> 101 us
    psum x1 -> x2, blocking collectives: 115 us -> 57.3 us  [the longest x1 52.4 us: per_device(): lax.psum(lax.psum(jnp.sum(grad_local * normed, axis=0), 'dp'), 'seq')]
  transfers between devices with their start and end apart: 8 -> 8, of which waited for: 2 -> 2; matrix products, arithmetic and copies ran while one was open for 1% -> 2% of each run, Pallas kernels for 0% -> 0%
where the time goes in v1:
time: 168 us; the launch traced here: 166 us
  blocking collectives  101 us (60%)
  starting transfers between devices  16.4 us (10%)
  matrix products  15.2 us (9%)
  waiting for transfers between devices  14.9 us (9%)
  local copies, waits for them, and re-layouts  10.8 us (6%)
  other arithmetic  5.26 us (3%)
  between operations  2.34 us (1%)
    psum x1, blocking collectives, per_device(): lax.psum(lax.psum(jnp.sum(grad_local * normed, axis=0), 'dp'), 'seq')  52.4 us
    psum x1, blocking collectives, per_device(): cross_total = lax.psum(cross_local, 'tensor')  23.3 us
    psum x1, blocking collectives, per_device(): square_total = lax.psum(square_local, 'tensor')  20.7 us
    ppermute x8, starting transfers between devices, shifted(): return lax.ppermute(array, axis, pairs)  16.4 us
    ppermute x8, waiting for transfers between devices, shifted(): return lax.ppermute(array, axis, pairs)  14.9 us
    unnamed x43, local copies, waits for them, and re-layouts  8.52 us
    psum x1, blocking collectives, per_device(): lax.psum(jnp.sum(grad_local * normed, axis=0), 'dp')  4.91 us
    dot_general x4, matrix products, per_device(): lax.dot_general(probs_b, grad_head, (((0,), (0,)), ((), ())), preferred_e...  4.21 us
  transfers between devices with their start and end apart: 8, of which 2 were waited for; matrix products, arithmetic and copies ran while one was open for 2% of the time, Pallas kernels for 0%

profile of v1, /device:TPU:6, one launch (start us, length us, event | category | flops | bytes accessed | tf_op | source)
XLA Modules:
  0.0 166.2 jit_solution(12098283196229241054)
XLA Ops:
  0.7 1.0 constant_dynamic-update-slice_fusion.1
  1.7 1.0 constant_dynamic-update-slice_fusion
  2.6 3.8 %collective-permute-start = (bf16[2,256,384]{2,1,0:T(8,128)(2,1)S(1)}, bf16[2,256,384]{2,1,0:T(8,128)(2,1)S(1)}, u32[]{:S(2)}, u32[]{:S(2)}) collective-permute-start(bf16[2,256,384]{2,1,0:T(8,128)(2,1)S(1)} %constant_dynamic-update-slice_fusion), channel_id=1, source_target_pairs={{0,16},{8,24},{16,32},{24,40},{32,48},{40,56},{48,64},{56,72},{64,... | collective-permute-start | bytes 1179656 | tf_op jit(solution)/shard_map/ppermute | solution.py:17
  6.5 1.5 collective-permute-start.1
  8.0 1.3 collective-permute-start.2
  9.3 1.3 collective-permute-start.3
  11.9 1.0 copy.12
  12.9 3.0 %collective-permute-done = bf16[2,256,384]{2,1,0:T(8,128)(2,1)S(1)} collective-permute-done((bf16[2,256,384]{2,1,0:T(8,128)(2,1)S(1)}, bf16[2,256,384]{2,1,0:T(8,128)(2,1)S(1)}, u32[]{:S(2)}, u32[]{:S(2)}) %collective-permute-start) | collective-permute-done | bytes 393248 | tf_op jit(solution)/shard_map/ppermute | solution.py:17
  16.2 11.9 %collective-permute-done.3 = bf16[2,256,384]{2,1,0:T(8,128)(2,1)S(1)} collective-permute-done((bf16[2,256,384]{2,1,0:T(8,128)(2,1)S(1)}, bf16[2,256,384]{2,1,0:T(8,128)(2,1)S(1)}, u32[]{:S(2)}, u32[]{:S(2)}) %collective-permute-start.3) | collective-permute-done | bytes 393248 | tf_op jit(solution)/shard_map/ppermute | solution.py:17
  33.1 20.7 %psum.28 = f32[128]{0:T(128)S(1)} all-reduce(f32[128]{0:T(128)S(1)} %multiply_reduce_fusion), channel_id=1, replica_groups=mesh['dp'=2,'seq'=32,'tensor'=8] {'tensor'}, use_global_device_ids=true, to_apply=%region_9.10 | all-reduce | flops 128 | bytes 1024 | tf_op jit(solution)/shard_map/psum | solution.py:79
  54.1 23.3 %psum.29 = f32[128]{0:T(128)S(1)} all-reduce(f32[128]{0:T(128)S(1)} %get-tuple-element.11), channel_id=1, replica_groups=mesh['dp'=2,'seq'=32,'tensor'=8] {'tensor'}, use_global_device_ids=true, to_apply=%region_11.12 | all-reduce | flops 128 | bytes 1024 | tf_op jit(solution)/shard_map/psum | solution.py:83
  77.5 1.4 fusion.19
  79.3 1.2 fusion.23
  80.5 1.1 fusion.25
  83.1 1.2 convolution_multiply_fusion.5
  84.3 1.1 fusion.70
  85.3 1.1 fusion.69
  86.4 1.0 fusion.68
  87.4 1.1 fusion.67
  89.4 1.2 fusion.24
  91.8 0.9 copy-done.11
  93.6 0.9 copy-done
  94.5 1.0 fusion.98
  95.6 3.8 %collective-permute-start.7 = (bf16[2,256,384]{1,2,0:T(8,128)(2,1)}, bf16[2,256,384]{1,2,0:T(8,128)(2,1)S(1)}, u32[]{:S(2)}, u32[]{:S(2)}) collective-permute-start(bf16[2,256,384]{1,2,0:T(8,128)(2,1)} %get-tuple-element.13), channel_id=1, source_target_pairs={{0,16},{8,24},{16,32},{24,40},{32,48},{40,56},{48,64},{56,72},{64,... | collective-permute-start | bytes 1179656 | tf_op jit(solution)/shard_map/ppermute | solution.py:17
  99.4 2.1 %collective-permute-start.6 = (bf16[2,256,384]{1,2,0:T(8,128)(2,1)}, bf16[2,256,384]{1,2,0:T(8,128)(2,1)}, u32[]{:S(2)}, u32[]{:S(2)}) collective-permute-start(bf16[2,256,384]{1,2,0:T(8,128)(2,1)} %get-tuple-element.14), channel_id=1, source_target_pairs={{0,8},{8,16},{16,24},{24,32},{32,40},{40,48},{48,56},{56,64},{64,7... | collective-permute-start | bytes 1179656 | tf_op jit(solution)/shard_map/ppermute | solution.py:17
  101.5 1.3 collective-permute-start.5
  102.8 1.3 collective-permute-start.4
  105.6 4.9 %psum.30 = f32[384]{0:T(512)S(1)} all-reduce(f32[384]{0:T(512)S(1)} %get-tuple-element.10), channel_id=1, replica_groups=mesh['dp'=2,'seq'=32,'tensor'=8] {'dp'}, use_global_device_ids=true, to_apply=%region_17.18 | all-reduce | flops 384 | bytes 3072 | tf_op jit(solution)/shard_map/psum | solution.py:88
  110.5 52.4 %psum.31 = f32[384]{0:T(512)} all-reduce(f32[384]{0:T(512)S(1)} %psum.30), channel_id=1, replica_groups=mesh['dp'=2,'seq'=32,'tensor'=8] {'seq'}, use_global_device_ids=true, to_apply=%region_18.19 | all-reduce | flops 384 | bytes 3072 | tf_op jit(solution)/shard_map/psum | solution.py:88
  162.9 1.6 fusion.18
  164.5 0.8 copy.23
  165.3 0.8 copy.24
  (80 shorter events, 11.9 us)
Async XLA Ops:
  0.6 15.4 %copy-start.7 = (bf16[1,256,384]{2,1,0:T(8,128)(2,1)S(1)}, bf16[1,256,384]{2,1,0:T(8,128)(2,1)}, u32[]{:S(2)}) copy-start(bf16[1,256,384]{2,1,0:T(8,128)(2,1)} %param.8) | copy-start | bytes 589828
  0.6 15.5 %copy-start.8 = (bf16[1,256,384]{2,1,0:T(8,128)(2,1)S(1)}, bf16[1,256,384]{2,1,0:T(8,128)(2,1)}, u32[]{:S(2)}) copy-start(bf16[1,256,384]{2,1,0:T(8,128)(2,1)} %param.9) | copy-start | bytes 589828
  2.6 13.3 %collective-permute-start = (bf16[2,256,384]{2,1,0:T(8,128)(2,1)S(1)}, bf16[2,256,384]{2,1,0:T(8,128)(2,1)S(1)}, u32[]{:S(2)}, u32[]{:S(2)}) collective-permute-start(bf16[2,256,384]{2,1,0:T(8,128)(2,1)S(1)} %constant_dynamic-update-slice_fusion), channel_id=1, source_target_pairs={{0,16},{8,24},{16,32},{24,40},{32,48},{40,56},{48,64},{56,72},{64,... | collective-permute-start | bytes 1179656 | tf_op jit(solution)/shard_map/ppermute | solution.py:17
  6.5 9.5 %collective-permute-start.1 = (bf16[2,256,384]{2,1,0:T(8,128)(2,1)S(1)}, bf16[2,256,384]{2,1,0:T(8,128)(2,1)S(1)}, u32[]{:S(2)}, u32[]{:S(2)}) collective-permute-start(bf16[2,256,384]{2,1,0:T(8,128)(2,1)S(1)} %constant_dynamic-update-slice_fusion), channel_id=1, source_target_pairs={{0,8},{8,16},{16,24},{24,32},{32,40},{40,48},{48,56},{56,64},{64,7... | collective-permute-start | bytes 1179656 | tf_op jit(solution)/shard_map/ppermute | solution.py:17
  8.0 8.2 %collective-permute-start.2 = (bf16[2,256,384]{2,1,0:T(8,128)(2,1)S(1)}, bf16[2,256,384]{2,1,0:T(8,128)(2,1)S(1)}, u32[]{:S(2)}, u32[]{:S(2)}) collective-permute-start(bf16[2,256,384]{2,1,0:T(8,128)(2,1)S(1)} %constant_dynamic-update-slice_fusion), channel_id=1, source_target_pairs={{8,0},{16,8},{24,16},{32,24},{40,32},{48,40},{56,48},{64,56},{72,6... | collective-permute-start | bytes 1179656 | tf_op jit(solution)/shard_map/ppermute | solution.py:17
  9.3 18.8 %collective-permute-start.3 = (bf16[2,256,384]{2,1,0:T(8,128)(2,1)S(1)}, bf16[2,256,384]{2,1,0:T(8,128)(2,1)S(1)}, u32[]{:S(2)}, u32[]{:S(2)}) collective-permute-start(bf16[2,256,384]{2,1,0:T(8,128)(2,1)S(1)} %constant_dynamic-update-slice_fusion), channel_id=1, source_target_pairs={{16,0},{24,8},{32,16},{40,24},{48,32},{56,40},{64,48},{72,56},{80,... | collective-permute-start | bytes 1179656 | tf_op jit(solution)/shard_map/ppermute | solution.py:17
  28.2 0.9 copy-start.9
  28.4 2.3 %copy-start.1 = (bf16[1280,384]{1,0:T(8,128)(2,1)}, bf16[1280,384]{1,0:T(8,128)(2,1)S(1)}, u32[]{:S(2)}) copy-start(bf16[1280,384]{1,0:T(8,128)(2,1)S(1)} %get-tuple-element.16) | copy-start | bytes 2949124
  28.4 4.3 %copy-start.5 = (bf16[1280,384]{1,0:T(8,128)(2,1)}, bf16[1280,384]{1,0:T(8,128)(2,1)S(1)}, u32[]{:S(2)}) copy-start(bf16[1280,384]{1,0:T(8,128)(2,1)S(1)} %get-tuple-element.17) | copy-start | bytes 2949124
  32.5 21.3 %copy-start.15 = (f32[384]{0:T(512)S(1)}, f32[384]{0:T(512)}, u32[]{:S(2)}) copy-start(f32[384]{0:T(512)} %param.11) | copy-start | bytes 4612
  77.3 1.6 copy-start.6
  80.5 1.3 copy-start.2
  88.5 2.5 %copy-start.10 = (f32[128,1280]{0,1:T(8,128)S(1)}, f32[128,1280]{0,1:T(8,128)}, u32[]{:S(2)}) copy-start(f32[128,1280]{0,1:T(8,128)} %get-tuple-element.35) | copy-start | bytes 1966084
  90.6 1.0 copy-start.4
  91.6 1.0 copy-start.11
  91.6 1.2 copy-start.12
  91.6 1.3 copy-start.13
  91.6 1.5 copy-start.14
  93.2 1.3 copy-start
  94.5 9.5 %copy-start.3 = (bf16[1280,384]{1,0:T(8,128)(2,1)S(1)}, bf16[1280,384]{1,0:T(8,128)(2,1)}, u32[]{:S(2)}) copy-start(bf16[1280,384]{1,0:T(8,128)(2,1)} %copy-done.1) | copy-start | bytes 2949124
  95.6 67.3 %collective-permute-start.7 = (bf16[2,256,384]{1,2,0:T(8,128)(2,1)}, bf16[2,256,384]{1,2,0:T(8,128)(2,1)S(1)}, u32[]{:S(2)}, u32[]{:S(2)}) collective-permute-start(bf16[2,256,384]{1,2,0:T(8,128)(2,1)} %get-tuple-element.13), channel_id=1, source_target_pairs={{0,16},{8,24},{16,32},{24,40},{32,48},{40,56},{48,64},{56,72},{64,... | collective-permute-start | bytes 1179656 | tf_op jit(solution)/shard_map/ppermute | solution.py:17
  99.4 63.5 %collective-permute-start.6 = (bf16[2,256,384]{1,2,0:T(8,128)(2,1)}, bf16[2,256,384]{1,2,0:T(8,128)(2,1)}, u32[]{:S(2)}, u32[]{:S(2)}) collective-permute-start(bf16[2,256,384]{1,2,0:T(8,128)(2,1)} %get-tuple-element.14), channel_id=1, source_target_pairs={{0,8},{8,16},{16,24},{24,32},{32,40},{40,48},{48,56},{56,64},{64,7... | collective-permute-start | bytes 1179656 | tf_op jit(solution)/shard_map/ppermute | solution.py:17
  101.5 61.4 %collective-permute-start.5 = (bf16[2,256,384]{1,2,0:T(8,128)(2,1)}, bf16[2,256,384]{1,2,0:T(8,128)(2,1)}, u32[]{:S(2)}, u32[]{:S(2)}) collective-permute-start(bf16[2,256,384]{1,2,0:T(8,128)(2,1)} %get-tuple-element.15), channel_id=1, source_target_pairs={{8,0},{16,8},{24,16},{32,24},{40,32},{48,40},{56,48},{64,56},{72,6... | collective-permute-start | bytes 1179656 | tf_op jit(solution)/shard_map/ppermute | solution.py:17
  102.8 60.1 %collective-permute-start.4 = (bf16[2,256,384]{1,2,0:T(8,128)(2,1)S(1)}, bf16[2,256,384]{1,2,0:T(8,128)(2,1)}, u32[]{:S(2)}, u32[]{:S(2)}) collective-permute-start(bf16[2,256,384]{1,2,0:T(8,128)(2,1)S(1)} %get-tuple-element.12), channel_id=1, source_target_pairs={{16,0},{24,8},{32,16},{40,24},{48,32},{56,40},{64,48},{72,56},{80,... | collective-permute-start | bytes 1179656 | tf_op jit(solution)/shard_map/ppermute | solution.py:17
